TPU v7x, 32 devices: a whole 2x2x4 slice. The times are simulated.
32 devices in a mesh: group: 4 (over y, x), seq: 4 (over z), hid: 2 (over core).
Axes of the slice: x: 2, y: 2, z: 4, core: 2. Of those that a mesh axis runs over, the one named last changes fastest.
Arguments:
- tokens: bfloat16 [4, 8192, 1280], P('group', ('seq', 'hid')), may hold values from -6 to 6
- slot_embed: bfloat16 [1280, 16], replicated, may hold values from -6 to 6
- seq_lengths: int32 [4, 8], P('group'), may hold values from 1 to 2048, 8192 in all within a row
- w_in: bfloat16 [8, 1280, 2560], P(('seq', 'hid'), None, 'group'), may hold values from -0.3125 to 0.3125
- w_out: bfloat16 [8, 2560, 1280], P(('seq', 'hid'), 'group'), may hold values from -0.25 to 0.25
Outputs:
- mixed: bfloat16 [4, 8192, 1280], P('group', ('seq', 'hid'))
Inputs may be any that keep to these rules, and one draw needn't show every extreme that they name: `seq_lengths`: each row sums to 8192; its largest entry is 2048.
All inputs are finite; a program needn't handle non-finite values.
Results may differ from a plain program's by a relative error of at most 0.013.
Values may be sent and summed in bfloat16 or wider, within the bound.
No kernel may reach another device: no remote copies, remote signals or barrier semaphores. Data moves between devices by JAX's collectives and lax.ppermute only.
A program may use at most 64 MiB of HBM per device.

v0:
```python
import jax
import jax.numpy as jnp
from jax import lax
from jax.sharding import PartitionSpec as P


def body(tokens, slot_embed, seq_lengths, w_in, w_out):
    local_tokens = tokens[0]
    tok_count = local_tokens.shape[0]
    shard_index = lax.axis_index("seq") * lax.axis_size("hid") + lax.axis_index("hid")
    position = shard_index * tok_count + jnp.arange(tok_count, dtype=jnp.int32)
    seq_end = jnp.cumsum(seq_lengths[0])
    seq_start = seq_end - seq_lengths[0]
    member = (position[:, None] >= seq_start[None, :]) & (position[:, None] < seq_end[None, :])
    member_f = member.astype(jnp.float32)
    seq_count = member.shape[1]
    highest = lax.Precision.HIGHEST
    logits = jnp.dot(local_tokens, slot_embed, preferred_element_type=jnp.float32)
    slot_count = logits.shape[1]
    masked = jnp.where(member[:, :, None], logits[:, None, :], -1e30)
    local_peak = jnp.max(masked, axis=0)
    seq_peak = lax.pmax(local_peak, ("seq", "hid"))
    token_peak = jnp.dot(member_f, seq_peak, precision=highest)
    exponent = jnp.exp(logits - token_peak)
    seq_total = lax.psum(jnp.dot(member_f.T, exponent, precision=highest), ("seq", "hid"))
    token_total = jnp.dot(member_f, seq_total, precision=highest)
    weights = exponent / token_total
    dispatch = (
        (weights[:, :, None] * member_f[:, None, :])
        .astype(jnp.bfloat16)
        .reshape(tok_count, slot_count * seq_count)
    )
    columns = dispatch
    own_rows = lax.psum_scatter(
        lax.dot_general(
            columns, local_tokens, (((0,), (0,)), ((), ())), preferred_element_type=jnp.float32
        ),
        ("seq", "hid"),
        scatter_dimension=0,
        tiled=True,
    )
    slot_inputs = own_rows.astype(jnp.bfloat16)
    hidden = jax.nn.gelu(
        jnp.dot(
            lax.all_gather(slot_inputs, "group", axis=0, tiled=True),
            w_in[0],
            preferred_element_type=jnp.float32,
        ),
        approximate=True,
    ).astype(jnp.bfloat16)
    partial_out = jnp.dot(hidden, w_out[0], preferred_element_type=jnp.float32)
    slot_outputs = lax.psum_scatter(
        partial_out.astype(jnp.bfloat16), "group", scatter_dimension=0, tiled=True
    )
    mix_weights = jax.nn.softmax(logits, axis=1)
    slot_table = (
        (mix_weights[:, :, None] * member_f[:, None, :])
        .astype(jnp.bfloat16)
        .reshape(tok_count, slot_count * seq_count)
    )
    block_rows = lax.all_gather(slot_outputs[None], ("seq", "hid"), axis=0, tiled=True)
    col_width = block_rows.shape[0] * block_rows.shape[1]
    columns = slot_table
    mixed = jnp.dot(
        columns,
        block_rows.reshape(col_width, block_rows.shape[2]),
        preferred_element_type=jnp.float32,
    )
    return mixed.astype(jnp.bfloat16)[None]


def solution(mesh):
    placed = (
        P("group", ("seq", "hid"), None),
        P(),
        P("group", None),
        P(("seq", "hid"), None, "group"),
        P(("seq", "hid"), "group", None),
    )
    return jax.shard_map(
        body,
        mesh=mesh,
        in_specs=placed,
        out_specs=P("group", ("seq", "hid"), None),
        check_vma=False,
    )
```

profile of v0, /device:TPU:0, one launch (start us, length us, event | category | flops | bytes accessed | tf_op | source)
XLA Modules:
  0.0 132.2 jit_solution(14160902849086294041)
XLA Ops:
  6.5 0.0 copy-start
  6.5 0.0 reduce-scatter.3.cloned.1.call-start
  6.5 1.0 reduce-window.4
  7.5 0.7 fusion.37
  8.2 0.1 copy-done
  8.3 1.6 %fusion.44 = (f32[1024]{0:T(1024)S(1)}, f32[1024,16]{0,1:T(8,128)S(1)}) fusion(bf16[1280,16]{0,1:T(8,128)(2,1)} %param.6, bf16[1,1024,1280]{2,1,0:T(8,128)(2,1)S(1)} %copy-done), kind=kOutput, calls=%fused_computation.48 | convolution fusion | flops 41958400 | bytes 2732032 | tf_op jit(solution)/shard_map/dot_general | solution.py:18
  9.9 0.1 fusion.43
  10.0 0.1 select_reduce_fusion
  10.1 18.1 %pmax.7 = f32[8,16]{1,0:T(8,128)S(1)} all-reduce(f32[8,16]{1,0:T(8,128)S(1)} %select_reduce_fusion), channel_id=1, replica_groups=mesh['group'=4,'seq'=4,'hid'=2] {'seq','hid'}, use_global_device_ids=true, to_apply=%region_4.5 | all-reduce | flops 128 | bytes 1024 | tf_op jit(solution)/shard_map/pmax | solution.py:22
  28.2 0.3 fusion.8
  28.5 0.2 fusion.42
  28.6 13.6 %psum.7 = f32[8,16]{1,0:T(8,128)S(1)} all-reduce(f32[8,16]{1,0:T(8,128)S(1)} %fusion.42), channel_id=1, replica_groups=mesh['group'=4,'seq'=4,'hid'=2] {'seq','hid'}, use_global_device_ids=true, to_apply=%region_5.6 | all-reduce | flops 128 | bytes 1024 | tf_op jit(solution)/shard_map/psum | solution.py:25
  42.3 0.3 convolution_divide_fusion
  42.5 1.4 %fusion.1 = f32[128,1280]{1,0:T(8,128)} fusion(bf16[1,1024,1280]{2,1,0:T(8,128)(2,1)S(1)} %copy-done, f32[1024,16]{0,1:T(8,128)S(1)} %convolution_divide_fusion, f32[1024,8]{0,1:T(8,128)S(1)} %get-tuple-element.5), kind=kOutput, calls=%fused_computation.2 | convolution fusion | flops 335806464 | bytes 3375104 | tf_op jit(solution)/shard_map/dot_general | solution.py:35
  43.9 0.0 reduce-scatter.3.cloned.1.call-update
  43.9 0.0 reduce-scatter.5.cloned.1.call-start
  43.9 29.9 %reduce-scatter.3.cloned.1.call-done = f32[16,1280]{1,0:T(8,128)} async-done(((f32[128,1280]{1,0:T(8,128)}), f32[16,1280]{1,0:T(8,128)}) %reduce-scatter.3.cloned.1.call-update) | async-done | bytes 81936 | tf_op jit(solution)/shard_map/reduce_scatter | solution.py:34
  73.9 0.9 convert_element_type.50
  74.8 8.7 %all_gather.6 = bf16[64,1280]{1,0:T(8,128)(2,1)S(1)} all-gather(bf16[16,1280]{1,0:T(8,128)(2,1)S(1)} %convert_element_type.50), channel_id=1, replica_groups=mesh['group'=4,'seq'=4,'hid'=2] {'group'}, dimensions={0}, use_global_device_ids=true | all-gather | bytes 204800 | tf_op jit(solution)/shard_map/all_gather | solution.py:45
  83.4 3.4 %convolution_convert_fusion.1 = bf16[64,1280]{1,0:T(8,128)(2,1)} fusion(bf16[1,640,1280]{2,1,0:T(8,128)(2,1)} %param.9, bf16[64,1280]{1,0:T(8,128)(2,1)S(1)} %all_gather.6, bf16[1,1280,640]{2,1,0:T(8,128)(2,1)} %param.8), kind=kOutput, calls=%fused_computation.6 | convolution fusion | flops 210165760 | bytes 3604480 | tf_op jit(solution)/shard_map/dot_general | solution.py:51
  86.8 0.0 reduce-scatter.5.cloned.1.call-update
  86.9 21.5 %reduce-scatter.5.cloned.1.call-done = bf16[16,1280]{1,0:T(8,128)(2,1)} async-done(((bf16[64,1280]{1,0:T(8,128)(2,1)}), bf16[16,1280]{1,0:T(8,128)(2,1)}) %reduce-scatter.5.cloned.1.call-update) | async-done | bytes 40976 | tf_op jit(solution)/shard_map/reduce_scatter | solution.py:52
  108.5 14.6 %all-gather = bf16[128,1280]{1,0:T(8,128)(2,1)S(1)} all-gather(bf16[16,1280]{1,0:T(8,128)(2,1)} %reduce-scatter.5.cloned.1.call-done), channel_id=2, replica_groups=mesh['group'=4,'seq'=4,'hid'=2] {'seq','hid'}, dimensions={0}, use_global_device_ids=true | all-gather | bytes 368640 | tf_op jit(solution)/shard_map/all_gather | solution.py:61
  123.0 2.4 %fusion = bf16[1,1024,1280]{2,1,0:T(8,128)(2,1)} fusion(bf16[128,1280]{1,0:T(8,128)(2,1)S(1)} %all-gather, f32[1024,8]{0,1:T(8,128)S(1)} %get-tuple-element.5, f32[1024,16]{0,1:T(8,128)S(1)} %fusion.35), kind=kOutput, calls=%fused_computation.1 | convolution fusion | flops 337117184 | bytes 3047424 | tf_op jit(solution)/shard_map/dot_general | solution.py:64
  (3 shorter events, 0.1 us)
Async XLA Ops:
  6.5 1.8 %copy-start = (bf16[1,1024,1280]{2,1,0:T(8,128)(2,1)S(1)}, bf16[1,1024,1280]{2,1,0:T(8,128)(2,1)}, u32[]{:S(2)}) copy-start(bf16[1,1024,1280]{2,1,0:T(8,128)(2,1)} %param.5) | copy-start | bytes 7864324
  6.5 67.3 %reduce-scatter.3.cloned.1.call-start = ((), (), s32[]{:S(2)}) async-start(), calls=%async_computation.2 | async-start | bytes 737280 | tf_op jit(solution)/shard_map/reduce_scatter | solution.py:34
  43.9 64.6 %reduce-scatter.5.cloned.1.call-start = ((), (), s32[]{:S(2)}) async-start(), calls=%async_computation.3 | async-start | bytes 204800 | tf_op jit(solution)/shard_map/reduce_scatter | solution.py:52
Sparse Core Ops, SparseCore 0:
  44.0 29.8 reduce-scatter.2
  87.0 21.4 reduce-scatter.4
where the time goes:
time: 133 us; the launch traced here: 132 us
  blocking collectives  55 us (41%)
  waiting for transfers between devices  51.5 us (39%)
  between operations  13.5 us (10%)
  matrix products  9.39 us (7%)
  other arithmetic  2.79 us (2%)
    reduce_scatter x1, waiting for transfers between devices, body(): lax.psum_scatter(lax.dot_general(columns, local_tokens, (((0,), (0,)), ((...  29.9 us
    reduce_scatter x1, waiting for transfers between devices, body(): lax.psum_scatter(partial_out.astype(jnp.bfloat16), 'group', scatter_dimen...  21.5 us
    pmax x1, blocking collectives, body(): seq_peak = lax.pmax(local_peak, ('seq', 'hid'))  18.1 us
    all_gather x1, blocking collectives, body(): lax.all_gather(slot_outputs[None], ('seq', 'hid'), axis=0, tiled=True)  14.6 us
    psum x1, blocking collectives, body(): lax.psum(jnp.dot(member_f.T, exponent, precision=highest), ('seq', 'hid'))  13.6 us
    all_gather x1, blocking collectives, body(): lax.all_gather(slot_inputs, 'group', axis=0, tiled=True)  8.66 us
    dot_general x1, matrix products, body(): partial_out = jnp.dot(hidden, w_out[0], preferred_element_type=jnp.float32)  3.4 us
  transfers between devices with their start and end apart: 2, of which 2 were waited for; matrix products, arithmetic and copies ran while one was open for 0% of the time, Pallas kernels for 0%

commit v1 on v0

--- a/solution.py
+++ b/solution.py
@@ -22,7 +22,9 @@
     seq_peak = lax.pmax(local_peak, ("seq", "hid"))
     token_peak = jnp.dot(member_f, seq_peak, precision=highest)
     exponent = jnp.exp(logits - token_peak)
-    seq_total = lax.psum(jnp.dot(member_f.T, exponent, precision=highest), ("seq", "hid"))
+    seq_total = jnp.sum(
+        lax.all_gather(jnp.dot(member_f.T, exponent, precision=highest), ("seq", "hid")), axis=0
+    )
     token_total = jnp.dot(member_f, seq_total, precision=highest)
     weights = exponent / token_total
     dispatch = (

time: 133 us -> 133 us (level)
    all_gather x0 -> x1, blocking collectives: none -> 14.1 us  [body(): lax.all_gather(jnp.dot(member_f.T, exponent, precision=highest), ('seq',...]
    psum x1 -> x0, blocking collectives: 13.6 us -> none  [body(): lax.psum(jnp.dot(member_f.T, exponent, precision=highest), ('seq', 'hid'))]
where the time goes in v1:
time: 133 us
  blocking collectives  55.5 us (42%)
  waiting for transfers between devices  51.4 us (39%)
  between operations  13.5 us (10%)
  matrix products  9.38 us (7%)
  other arithmetic  2.8 us (2%)
    reduce_scatter x1, waiting for transfers between devices, body(): lax.psum_scatter(lax.dot_general(columns, local_tokens, (((0,), (0,)), ((...  29.9 us
    reduce_scatter x1, waiting for transfers between devices, body(): lax.psum_scatter(partial_out.astype(jnp.bfloat16), 'group', scatter_dimen...  21.5 us
    pmax x1, blocking collectives, body(): seq_peak = lax.pmax(local_peak, ('seq', 'hid'))  18.1 us
    all_gather x1, blocking collectives, body(): lax.all_gather(slot_outputs[None], ('seq', 'hid'), axis=0, tiled=True)  14.6 us
    all_gather x1, blocking collectives, body(): lax.all_gather(jnp.dot(member_f.T, exponent, precision=highest), ('seq',...  14.1 us
    all_gather x1, blocking collectives, body(): lax.all_gather(slot_inputs, 'group', axis=0, tiled=True)  8.67 us
    dot_general x1, matrix products, body(): partial_out = jnp.dot(hidden, w_out[0], preferred_element_type=jnp.float32)  3.39 us
  transfers between devices with their start and end apart: 2, of which 2 were waited for; matrix products, arithmetic and copies ran while one was open for 0% of the time, Pallas kernels for 0%

profile of v1, /device:TPU:0, one launch (start us, length us, event | category | flops | bytes accessed | tf_op | source)
XLA Modules:
  0.0 132.7 jit_solution(4319129441120626156)
XLA Ops:
  6.5 0.0 copy-start
  6.5 0.0 reduce-scatter.3.cloned.1.call-start
  6.5 1.0 reduce-window.4
  7.5 0.7 fusion.37
  8.2 0.1 copy-done
  8.3 1.6 %fusion.44 = (f32[1024]{0:T(1024)S(1)}, f32[1024,16]{0,1:T(8,128)S(1)}) fusion(bf16[1280,16]{0,1:T(8,128)(2,1)} %param.6, bf16[1,1024,1280]{2,1,0:T(8,128)(2,1)S(1)} %copy-done), kind=kOutput, calls=%fused_computation.49 | convolution fusion | flops 41958400 | bytes 2732032 | tf_op jit(solution)/shard_map/dot_general | solution.py:18
  9.9 0.1 fusion.43
  10.0 0.1 select_reduce_fusion
  10.1 18.1 %pmax.7 = f32[8,16]{1,0:T(8,128)S(1)} all-reduce(f32[8,16]{1,0:T(8,128)S(1)} %select_reduce_fusion), channel_id=1, replica_groups=mesh['group'=4,'seq'=4,'hid'=2] {'seq','hid'}, use_global_device_ids=true, to_apply=%region_4.5 | all-reduce | flops 128 | bytes 1024 | tf_op jit(solution)/shard_map/pmax | solution.py:22
  28.2 0.3 fusion.8
  28.5 0.2 fusion.42
  28.6 14.1 %all-gather = f32[64,16]{1,0:T(8,128)S(1)} all-gather(f32[8,16]{1,0:T(8,128)S(1)} %fusion.42), channel_id=2, replica_groups=mesh['group'=4,'seq'=4,'hid'=2] {'seq','hid'}, dimensions={0}, use_global_device_ids=true | all-gather | bytes 4608 | tf_op jit(solution)/shard_map/all_gather | solution.py:26
  42.8 0.3 convolution_divide_fusion
  43.0 1.4 %fusion.1 = f32[128,1280]{1,0:T(8,128)} fusion(bf16[1,1024,1280]{2,1,0:T(8,128)(2,1)S(1)} %copy-done, f32[1024,16]{0,1:T(8,128)S(1)} %convolution_divide_fusion, f32[1024,8]{0,1:T(8,128)S(1)} %get-tuple-element.5), kind=kOutput, calls=%fused_computation.2 | convolution fusion | flops 335806464 | bytes 3375104 | tf_op jit(solution)/shard_map/dot_general | solution.py:37
  44.4 0.0 reduce-scatter.3.cloned.1.call-update
  44.4 0.0 reduce-scatter.5.cloned.1.call-start
  44.5 29.9 %reduce-scatter.3.cloned.1.call-done = f32[16,1280]{1,0:T(8,128)} async-done(((f32[128,1280]{1,0:T(8,128)}), f32[16,1280]{1,0:T(8,128)}) %reduce-scatter.3.cloned.1.call-update) | async-done | bytes 81936 | tf_op jit(solution)/shard_map/reduce_scatter | solution.py:36
  74.3 0.9 convert_element_type.50
  75.2 8.7 %all_gather.14 = bf16[64,1280]{1,0:T(8,128)(2,1)S(1)} all-gather(bf16[16,1280]{1,0:T(8,128)(2,1)S(1)} %convert_element_type.50), channel_id=1, replica_groups=mesh['group'=4,'seq'=4,'hid'=2] {'group'}, dimensions={0}, use_global_device_ids=true | all-gather | bytes 204800 | tf_op jit(solution)/shard_map/all_gather | solution.py:47
  83.9 3.4 %convolution_convert_fusion.1 = bf16[64,1280]{1,0:T(8,128)(2,1)} fusion(bf16[1,640,1280]{2,1,0:T(8,128)(2,1)} %param.9, bf16[64,1280]{1,0:T(8,128)(2,1)S(1)} %all_gather.14, bf16[1,1280,640]{2,1,0:T(8,128)(2,1)} %param.8), kind=kOutput, calls=%fused_computation.6 | convolution fusion | flops 210165760 | bytes 3604480 | tf_op jit(solution)/shard_map/dot_general | solution.py:53
  87.3 0.0 reduce-scatter.5.cloned.1.call-update
  87.4 21.5 %reduce-scatter.5.cloned.1.call-done = bf16[16,1280]{1,0:T(8,128)(2,1)} async-done(((bf16[64,1280]{1,0:T(8,128)(2,1)}), bf16[16,1280]{1,0:T(8,128)(2,1)}) %reduce-scatter.5.cloned.1.call-update) | async-done | bytes 40976 | tf_op jit(solution)/shard_map/reduce_scatter | solution.py:54
  108.9 14.6 %all-gather.1 = bf16[128,1280]{1,0:T(8,128)(2,1)S(1)} all-gather(bf16[16,1280]{1,0:T(8,128)(2,1)} %reduce-scatter.5.cloned.1.call-done), channel_id=3, replica_groups=mesh['group'=4,'seq'=4,'hid'=2] {'seq','hid'}, dimensions={0}, use_global_device_ids=true | all-gather | bytes 368640 | tf_op jit(solution)/shard_map/all_gather | solution.py:63
  123.5 2.4 %fusion = bf16[1,1024,1280]{2,1,0:T(8,128)(2,1)} fusion(bf16[128,1280]{1,0:T(8,128)(2,1)S(1)} %all-gather.1, f32[1024,8]{0,1:T(8,128)S(1)} %get-tuple-element.5, f32[1024,16]{0,1:T(8,128)S(1)} %fusion.35), kind=kOutput, calls=%fused_computation.1 | convolution fusion | flops 337117184 | bytes 3047424 | tf_op jit(solution)/shard_map/dot_general | solution.py:66
  (4 shorter events, 0.1 us)
Async XLA Ops:
  6.5 1.8 %copy-start = (bf16[1,1024,1280]{2,1,0:T(8,128)(2,1)S(1)}, bf16[1,1024,1280]{2,1,0:T(8,128)(2,1)}, u32[]{:S(2)}) copy-start(bf16[1,1024,1280]{2,1,0:T(8,128)(2,1)} %param.5) | copy-start | bytes 7864324
  6.5 67.8 %reduce-scatter.3.cloned.1.call-start = ((), (), s32[]{:S(2)}) async-start(), calls=%async_computation.2 | async-start | bytes 737280 | tf_op jit(solution)/shard_map/reduce_scatter | solution.py:36
  44.4 64.5 %reduce-scatter.5.cloned.1.call-start = ((), (), s32[]{:S(2)}) async-start(), calls=%async_computation.3 | async-start | bytes 204800 | tf_op jit(solution)/shard_map/reduce_scatter | solution.py:54
Sparse Core Ops, SparseCore 0:
  44.5 29.7 reduce-scatter.2
  87.4 21.4 reduce-scatter.4
